TPU v7x, 32 devices: a whole 2x2x4 slice. The times are simulated.
32 devices in a mesh: pat: 4 (over z), vox: 8 (over y, x, core).
Axes of the slice: x: 2, y: 2, z: 4, core: 2. Of those that a mesh axis runs over, the one named last changes fastest.
Arguments:
- conductivity: float32 [16, 128, 128], P('vox'), may hold values from 0.3 to 1.5
- warm_forward: float32 [16, 32, 128, 128], P('vox', 'pat'), may hold values from -3 to 3
- warm_adjoint: float32 [16, 32, 128, 128], P('vox', 'pat'), may hold values from -3 to 3
- electrodes: int32 [128], replicated, may hold values from 0 to 262143
- patterns: int32 [32, 4], P('pat'), may hold values from 0 to 127, all different within a row
- observed: float32 [32], P('pat'), may hold values from -16 to 16
Outputs:
- gradient: float32 [16, 128, 128], P('vox')
- predicted: float32 [32], P('pat')
All inputs are finite; a program needn't handle non-finite values.
Results may differ from a plain program's by a relative error of at most 0.0003.
Values sent between devices are 32-bit elements; how exact they have to be, the bound alone decides.
No kernel may reach another device: no remote copies, remote signals or barrier semaphores. Data moves between devices by JAX's collectives and lax.ppermute only.
A program may use at most 64 MiB of HBM per device.

v0:
```python
import math
import jax
import jax.numpy as jnp
from jax import lax
from jax.sharding import PartitionSpec as P

ITERS = 2
leakage = 0.05


def extended(block, sides, width):
    for axis, dim in sides:
        count = lax.axis_size(axis)
        forward = [(i, i + 1) for i in range(count - 1)]
        backward = [(target, source) for source, target in forward]
        low = lax.ppermute(
            lax.slice_in_dim(block, block.shape[dim] - width, None, axis=dim), axis, forward
        )
        high = lax.ppermute(lax.slice_in_dim(block, 0, width, axis=dim), axis, backward)
        block = jnp.concatenate([low, block, high], axis=dim)
    return block


def both_sides(values, along_axis):
    lower_pad = [(0, 0)] * values.ndim
    upper_pad = [(0, 0)] * values.ndim
    lower_pad[along_axis] = (1, 0)
    upper_pad[along_axis] = (0, 1)
    return jnp.pad(values, lower_pad) + jnp.pad(values, upper_pad)


def spread(values, along_axis):
    lower_pad = [(0, 0)] * values.ndim
    upper_pad = [(0, 0)] * values.ndim
    lower_pad[along_axis] = (1, 0)
    upper_pad[along_axis] = (0, 1)
    return jnp.pad(values, lower_pad) - jnp.pad(values, upper_pad)


def operate(values, coeffs):
    depth_faces, row_faces, column_faces = coeffs
    padded = extended(values, (("vox", 0),), 1)
    flux_depth = depth_faces[:, None] * (padded[1:] - padded[:-1])
    result = leakage * values + (flux_depth[:-1] - flux_depth[1:])
    result = result + spread(row_faces[:, None] * (values[:, :, 1:] - values[:, :, :-1]), 2)
    result = result + spread(
        column_faces[:, None] * (values[:, :, :, 1:] - values[:, :, :, :-1]), 3
    )
    return result


def inner(left_factor, right_factor):
    return jnp.sum(left_factor * right_factor, axis=(0, 2, 3))


def widen(vector):
    return vector[None, :, None, None]


def pattern_sum(local_terms):
    return lax.psum(local_terms, "vox")


def solve_pattern(right_side, initial, coeffs, diagonal):
    solution = initial
    residue = right_side - operate(solution, coeffs)
    precond = residue / diagonal
    direction = precond
    current = pattern_sum(inner(residue, precond))
    for iteration in range(ITERS):
        applied = operate(direction, coeffs)
        step_size = current / pattern_sum(inner(direction, applied))
        solution = solution + widen(step_size) * direction
        residue = residue - widen(step_size) * applied
        if iteration + 1 < ITERS:
            precond = residue / diagonal
            following = pattern_sum(inner(residue, precond))
            direction = precond + widen(following / current) * direction
            current = following
    return solution


def per_device(conductivity, warm_forward, warm_adjoint, electrodes, patterns, observed):
    plane_count, pattern_count, row_count, column_count = warm_forward.shape
    position = lax.axis_index("vox")
    layers = lax.axis_size("vox")
    strength = 2.0 * math.sqrt(layers * plane_count * row_count * column_count)
    data_weight = 0.1 * strength
    lower_open = (position > 0).astype(jnp.float32)
    upper_open = (position < layers - 1).astype(jnp.float32)
    padded_sigma = extended(conductivity, (("vox", 0),), 1)
    face_mask = jnp.concatenate(
        [lower_open[None], jnp.ones((plane_count - 1,), jnp.float32), upper_open[None]]
    )
    depth_faces = 0.5 * (padded_sigma[1:] + padded_sigma[:-1]) * face_mask[:, None, None]
    row_faces = 0.5 * (conductivity[:, 1:] + conductivity[:, :-1])
    column_faces = 0.5 * (conductivity[:, :, 1:] + conductivity[:, :, :-1])
    coeffs = (depth_faces, row_faces, column_faces)
    diagonal = (
        leakage
        + (depth_faces[:-1] + depth_faces[1:])
        + both_sides(row_faces, 1)
        + both_sides(column_faces, 2)
    )
    diagonal = diagonal[:, None]
    electrode_ids = jnp.arange(electrodes.shape[0], dtype=jnp.int32)
    picked = jnp.sum(
        jnp.where(
            patterns[:, :, None] == electrode_ids[None, None, :], electrodes[None, None, :], 0
        ),
        axis=2,
    )
    offset = position * (plane_count * row_count * column_count)
    local_cell = picked - offset
    grid_shape = (plane_count, 1, row_count, column_count)
    cell_index = (
        lax.broadcasted_iota(jnp.int32, grid_shape, 0) * row_count
        + lax.broadcasted_iota(jnp.int32, grid_shape, 2)
    ) * column_count + lax.broadcasted_iota(jnp.int32, grid_shape, 3)

    def marker(which_one):
        return (cell_index == local_cell[:, which_one][None, :, None, None]).astype(jnp.float32)

    forward = solve_pattern(strength * (marker(0) - marker(1)), warm_forward, coeffs, diagonal)
    probe_weights = marker(2) - marker(3)
    predicted = lax.psum(inner(probe_weights, forward), "vox")
    misfit = predicted - observed
    adjoint = solve_pattern(
        widen(data_weight * misfit) * probe_weights, warm_adjoint, coeffs, diagonal
    )
    stacked = jnp.concatenate([forward, adjoint], axis=1)
    padded_pair = extended(stacked, (("vox", 0),), 1)
    padded_forward = padded_pair[:, :pattern_count]
    padded_adjoint = padded_pair[:, pattern_count:]
    depth_products = jnp.sum(
        (padded_forward[1:] - padded_forward[:-1]) * (padded_adjoint[1:] - padded_adjoint[:-1]),
        axis=1,
    )
    depth_products = depth_products * face_mask[:, None, None]
    grad_depth = depth_products[:-1] + depth_products[1:]
    row_products = jnp.sum(
        (forward[:, :, 1:] - forward[:, :, :-1]) * (adjoint[:, :, 1:] - adjoint[:, :, :-1]), axis=1
    )
    column_products = jnp.sum(
        (forward[:, :, :, 1:] - forward[:, :, :, :-1])
        * (adjoint[:, :, :, 1:] - adjoint[:, :, :, :-1]),
        axis=1,
    )
    local_gradient = -0.5 * (
        grad_depth + both_sides(row_products, 1) + both_sides(column_products, 2)
    )
    gradient = lax.psum(local_gradient, "pat")
    return (gradient, predicted)


def solution(mesh):
    in_specs = (
        P("vox", None, None),
        P("vox", "pat", None, None),
        P("vox", "pat", None, None),
        P(),
        P("pat", None),
        P("pat"),
    )
    out_specs = (P("vox", None, None), P("pat"))
    return jax.shard_map(
        per_device, mesh=mesh, in_specs=in_specs, out_specs=out_specs, check_vma=False
    )
```

profile of v0, /device:TPU:0, one launch (start us, length us, event | category | flops | bytes accessed | tf_op | source)
XLA Modules:
  0.0 282.5 jit_solution(13601715273596078150)
XLA Ops:
  7.2 1.0 fusion.63
  8.2 1.3 collective-permute-start
  9.5 3.0 %collective-permute-start.1 = (f32[1,128,128]{2,1,0:T(8,128)S(1)}, f32[1,128,128]{2,1,0:T(8,128)S(1)}, u32[]{:S(2)}, u32[]{:S(2)}) collective-permute-start(f32[1,128,128]{2,1,0:T(8,128)S(1)} %get-tuple-element.42), channel_id=1, source_target_pairs={{0,1},{1,2},{2,3},{3,4},{4,5},{5,6},{6,7},{8,9},{9,10},{10,11},{11... | collective-permute-start | bytes 196616 | tf_op jit(solution)/shard_map/ppermute | solution.py:16
  12.5 2.1 fusion.61
  14.6 1.4 collective-permute-start.2
  16.1 5.9 %collective-permute-start.3 = (f32[1,8,128,128]{3,2,1,0:T(8,128)S(1)}, f32[1,8,128,128]{3,2,1,0:T(8,128)}, u32[]{:S(2)}, u32[]{:S(2)}) collective-permute-start(f32[1,8,128,128]{3,2,1,0:T(8,128)S(1)} %get-tuple-element.32), channel_id=1, source_target_pairs={{0,1},{1,2},{2,3},{3,4},{4,5},{5,6},{6,7},{8,9},{9,10},{10,11},{11... | collective-permute-start | bytes 1572872 | tf_op jit(solution)/shard_map/ppermute | solution.py:16
  22.0 1.1 fusion.62
  23.1 3.7 %collective-permute-start.9 = (f32[1,8,128,128]{3,2,1,0:T(8,128)}, f32[1,8,128,128]{3,2,1,0:T(8,128)}, u32[]{:S(2)}, u32[]{:S(2)}) collective-permute-start(f32[1,8,128,128]{3,2,1,0:T(8,128)} %get-tuple-element.34), channel_id=1, source_target_pairs={{0,1},{1,2},{2,3},{3,4},{4,5},{5,6},{6,7},{8,9},{9,10},{10,11},{11... | collective-permute-start | bytes 1572872 | tf_op jit(solution)/shard_map/ppermute | solution.py:16
  26.9 0.7 iota_add_fusion
  28.7 1.4 fusion.2
  30.1 0.8 broadcast_divide_fusion.1
  31.0 1.4 collective-permute-start.4
  32.5 3.3 %collective-permute-start.5 = (f32[1,8,128,128]{3,2,1,0:T(8,128)S(1)}, f32[1,8,128,128]{3,2,1,0:T(8,128)S(1)}, u32[]{:S(2)}, u32[]{:S(2)}) collective-permute-start(f32[1,8,128,128]{3,2,1,0:T(8,128)S(1)} %get-tuple-element.30), channel_id=1, source_target_pairs={{0,1},{1,2},{2,3},{3,4},{4,5},{5,6},{6,7},{8,9},{9,10},{10,11},{11... | collective-permute-start | bytes 1572872 | tf_op jit(solution)/shard_map/ppermute | solution.py:16
  36.4 1.0 collective-permute-done.5
  37.5 1.7 multiply_reduce_fusion.5
  39.2 27.2 %all-reduce.33 = (f32[8]{0:T(128)S(1)}, f32[8]{0:T(128)S(1)}) all-reduce(f32[8]{0:T(128)S(1)} %get-tuple-element.5, f32[8]{0:T(128)S(1)} %get-tuple-element.4), channel_id=1, replica_groups=mesh['pat'=4,'vox'=8] {'vox'}, use_global_device_ids=true, to_apply=%region_2.3 | all-reduce | flops 16 | bytes 128 | tf_op jit(solution)/shard_map/psum | solution.py:61
  66.5 1.6 multiply_reduce_fusion.4
  68.0 1.3 collective-permute-start.8
  69.3 15.8 %psum.72 = f32[8]{0:T(128)S(1)} all-reduce(f32[8]{0:T(128)S(1)} %multiply_reduce_fusion.4), channel_id=1, replica_groups=mesh['pat'=4,'vox'=8] {'vox'}, use_global_device_ids=true, to_apply=%region_6.7 | all-reduce | flops 8 | bytes 64 | tf_op jit(solution)/shard_map/psum | solution.py:61
  85.2 1.8 multiply_add_fusion.3
  87.1 1.3 collective-permute-start.6
  88.4 3.2 %collective-permute-start.7 = (f32[1,8,128,128]{3,2,1,0:T(8,128)S(1)}, f32[1,8,128,128]{3,2,1,0:T(8,128)S(1)}, u32[]{:S(2)}, u32[]{:S(2)}) collective-permute-start(f32[1,8,128,128]{3,2,1,0:T(8,128)S(1)} %get-tuple-element.28), channel_id=1, source_target_pairs={{0,1},{1,2},{2,3},{3,4},{4,5},{5,6},{6,7},{8,9},{9,10},{10,11},{11... | collective-permute-start | bytes 1572872 | tf_op jit(solution)/shard_map/ppermute | solution.py:16
  91.6 1.6 fusion.29
  93.2 1.3 fusion.30
  94.5 2.8 fusion.4
  98.0 20.6 %psum.73 = f32[8]{0:T(128)S(1)} all-reduce(f32[8]{0:T(128)S(1)} %fusion.35), channel_id=1, replica_groups=mesh['pat'=4,'vox'=8] {'vox'}, use_global_device_ids=true, to_apply=%region_8.9 | all-reduce | flops 8 | bytes 64 | tf_op jit(solution)/shard_map/psum | solution.py:61
  118.6 2.8 multiply_reduce_fusion.3
  121.4 12.4 %psum.74 = f32[8]{0:T(128)S(1)} all-reduce(f32[8]{0:T(128)S(1)} %get-tuple-element.15), channel_id=1, replica_groups=mesh['pat'=4,'vox'=8] {'vox'}, use_global_device_ids=true, to_apply=%region_10.11 | all-reduce | flops 8 | bytes 64 | tf_op jit(solution)/shard_map/psum | solution.py:126
  133.9 3.7 %broadcast_divide_fusion = (f32[2,8,128,128]{3,2,1,0:T(8,128)S(1)}, f32[2,8,128,128]{3,2,1,0:T(8,128)S(1)}) fusion(f32[2,128,128]{2,1,0:T(8,128)S(1)} %fusion.51, f32[2,8,128,127]{3,2,1,0:T(8,128)} %get-tuple-element.41, f32[2,8,127,128]{3,2,1,0:T(8,128)} %get-tuple-element.39, f32[3,8,128,128]{3,2,1,0:T(8,128)} %get-tuple-element.37, ...), kind=kLoop, calls=%fused_computation.94 | loop fusion | flops 3932160 | bytes 7585888 | tf_op jit(solution)/shard_map/div | solution.py:67
  137.7 1.3 collective-permute-start.10
  139.0 3.2 %collective-permute-start.11 = (f32[1,8,128,128]{3,2,1,0:T(8,128)S(1)}, f32[1,8,128,128]{3,2,1,0:T(8,128)S(1)}, u32[]{:S(2)}, u32[]{:S(2)}) collective-permute-start(f32[1,8,128,128]{3,2,1,0:T(8,128)S(1)} %get-tuple-element.26), channel_id=1, source_target_pairs={{0,1},{1,2},{2,3},{3,4},{4,5},{5,6},{6,7},{8,9},{9,10},{10,11},{11... | collective-permute-start | bytes 1572872 | tf_op jit(solution)/shard_map/ppermute | solution.py:16
  142.8 1.0 collective-permute-done.11
  143.9 0.8 multiply_reduce_fusion.1
  144.7 20.3 %all-reduce.32 = (f32[8]{0:T(128)S(1)}, f32[8]{0:T(128)S(1)}) all-reduce(f32[8]{0:T(128)S(1)} %get-tuple-element.3, f32[8]{0:T(128)S(1)} %get-tuple-element.2), channel_id=1, replica_groups=mesh['pat'=4,'vox'=8] {'vox'}, use_global_device_ids=true, to_apply=%region_12.13 | all-reduce | flops 16 | bytes 128 | tf_op jit(solution)/shard_map/psum | solution.py:61
  165.4 12.6 %psum.77 = f32[8]{0:T(128)S(1)} all-reduce(f32[8]{0:T(128)S(1)} %multiply_reduce_fusion), channel_id=1, replica_groups=mesh['pat'=4,'vox'=8] {'vox'}, use_global_device_ids=true, to_apply=%region_16.17 | all-reduce | flops 8 | bytes 64 | tf_op jit(solution)/shard_map/psum | solution.py:61
  178.0 1.5 multiply_add_fusion.1
  179.6 1.3 collective-permute-start.12
  180.9 3.2 %collective-permute-start.13 = (f32[1,8,128,128]{3,2,1,0:T(8,128)S(1)}, f32[1,8,128,128]{3,2,1,0:T(8,128)S(1)}, u32[]{:S(2)}, u32[]{:S(2)}) collective-permute-start(f32[1,8,128,128]{3,2,1,0:T(8,128)S(1)} %get-tuple-element.24), channel_id=1, source_target_pairs={{0,1},{1,2},{2,3},{3,4},{4,5},{5,6},{6,7},{8,9},{9,10},{10,11},{11... | collective-permute-start | bytes 1572872 | tf_op jit(solution)/shard_map/ppermute | solution.py:16
  184.7 1.0 collective-permute-done.13
  186.5 20.7 %psum.78 = f32[8]{0:T(128)S(1)} all-reduce(f32[8]{0:T(128)S(1)} %fusion.19), channel_id=1, replica_groups=mesh['pat'=4,'vox'=8] {'vox'}, use_global_device_ids=true, to_apply=%region_18.19 | all-reduce | flops 8 | bytes 64 | tf_op jit(solution)/shard_map/psum | solution.py:61
  207.5 0.9 copy-done.2
  208.7 1.3 collective-permute-start.14
  210.0 3.1 %collective-permute-start.15 = (f32[1,16,128,128]{3,2,1,0:T(8,128)S(1)}, f32[1,16,128,128]{3,2,1,0:T(8,128)S(1)}, u32[]{:S(2)}, u32[]{:S(2)}) collective-permute-start(f32[1,16,128,128]{3,2,1,0:T(8,128)S(1)} %get-tuple-element.23), channel_id=1, source_target_pairs={{0,1},{1,2},{2,3},{3,4},{4,5},{5,6},{6,7},{8,9},{9,10},{10,11},{11... | collective-permute-start | bytes 3145736 | tf_op jit(solution)/shard_map/ppermute | solution.py:16
  214.0 1.3 collective-permute-done.15
  215.3 0.8 pad_maximum_fusion
  216.9 0.8 fusion.48
  217.7 56.4 %all-reduce.36.cloned.1.call-done = f32[2,128,128]{2,1,0:T(8,128)} async-done(((f32[2,128,128]{2,1,0:T(8,128)}), f32[2,128,128]{2,1,0:T(8,128)}) %all-reduce.36.cloned.1.call-update) | async-done | bytes 131088 | tf_op jit(solution)/shard_map/psum | solution.py:152
  274.0 1.6 copy.10
  (96 shorter events, 7.5 us)
Async XLA Ops:
  7.2 14.8 %copy-start = (f32[2,8,128,128]{3,2,1,0:T(8,128)S(1)}, f32[2,8,128,128]{3,2,1,0:T(8,128)}, u32[]{:S(2)}) copy-start(f32[2,8,128,128]{3,2,1,0:T(8,128)} %param.8) | copy-start | bytes 3145732
  7.2 266.9 %all-reduce.36.cloned.1.call-start = ((), (), s32[]{:S(2)}) async-start(), calls=%async_computation | async-start | bytes 262144 | tf_op jit(solution)/shard_map/psum | solution.py:152
  8.2 20.3 %collective-permute-start = (f32[1,128,128]{2,1,0:T(8,128)S(1)}, f32[1,128,128]{2,1,0:T(8,128)S(1)}, u32[]{:S(2)}, u32[]{:S(2)}) collective-permute-start(f32[1,128,128]{2,1,0:T(8,128)S(1)} %get-tuple-element.43), channel_id=1, source_target_pairs={{1,0},{2,1},{3,2},{4,3},{5,4},{6,5},{7,6},{9,8},{10,9},{11,10},{12... | collective-permute-start | bytes 196616 | tf_op jit(solution)/shard_map/ppermute | solution.py:19
  9.5 19.0 %collective-permute-start.1 = (f32[1,128,128]{2,1,0:T(8,128)S(1)}, f32[1,128,128]{2,1,0:T(8,128)S(1)}, u32[]{:S(2)}, u32[]{:S(2)}) collective-permute-start(f32[1,128,128]{2,1,0:T(8,128)S(1)} %get-tuple-element.42), channel_id=1, source_target_pairs={{0,1},{1,2},{2,3},{3,4},{4,5},{5,6},{6,7},{8,9},{9,10},{10,11},{11... | collective-permute-start | bytes 196616 | tf_op jit(solution)/shard_map/ppermute | solution.py:16
  14.6 12.1 %copy-start.15 = (f32[2,128,128]{2,1,0:T(8,128)S(1)}, f32[2,128,128]{2,1,0:T(8,128)}, u32[]{:S(2)}) copy-start(f32[2,128,128]{2,1,0:T(8,128)} %param.6) | copy-start | bytes 393220
  14.6 13.0 %copy-start.17 = (s32[8,4]{0,1:T(4,128)S(1)}, s32[8,4]{0,1:T(4,128)}, u32[]{:S(2)}) copy-start(s32[8,4]{0,1:T(4,128)} %param.10) | copy-start | bytes 388
  14.6 13.0 %copy-start.18 = (s32[128]{0:T(128)S(1)}, s32[128]{0:T(128)}, u32[]{:S(2)}) copy-start(s32[128]{0:T(128)} %param.9) | copy-start | bytes 1540
  14.6 13.3 %copy-start.1 = (f32[2,8,128,128]{3,2,1,0:T(8,128)S(1)}, f32[2,8,128,128]{3,2,1,0:T(8,128)}, u32[]{:S(2)}) copy-start(f32[2,8,128,128]{3,2,1,0:T(8,128)} %param.7) | copy-start | bytes 3145732
  14.6 14.1 %collective-permute-start.2 = (f32[1,8,128,128]{3,2,1,0:T(8,128)}, f32[1,8,128,128]{3,2,1,0:T(8,128)}, u32[]{:S(2)}, u32[]{:S(2)}) collective-permute-start(f32[1,8,128,128]{3,2,1,0:T(8,128)} %get-tuple-element.33), channel_id=1, source_target_pairs={{1,0},{2,1},{3,2},{4,3},{5,4},{6,5},{7,6},{9,8},{10,9},{11,10},{12... | collective-permute-start | bytes 1572872 | tf_op jit(solution)/shard_map/ppermute | solution.py:19
  16.1 12.7 %collective-permute-start.3 = (f32[1,8,128,128]{3,2,1,0:T(8,128)S(1)}, f32[1,8,128,128]{3,2,1,0:T(8,128)}, u32[]{:S(2)}, u32[]{:S(2)}) collective-permute-start(f32[1,8,128,128]{3,2,1,0:T(8,128)S(1)} %get-tuple-element.32), channel_id=1, source_target_pairs={{0,1},{1,2},{2,3},{3,4},{4,5},{5,6},{6,7},{8,9},{9,10},{10,11},{11... | collective-permute-start | bytes 1572872 | tf_op jit(solution)/shard_map/ppermute | solution.py:16
  23.1 71.4 %collective-permute-start.9 = (f32[1,8,128,128]{3,2,1,0:T(8,128)}, f32[1,8,128,128]{3,2,1,0:T(8,128)}, u32[]{:S(2)}, u32[]{:S(2)}) collective-permute-start(f32[1,8,128,128]{3,2,1,0:T(8,128)} %get-tuple-element.34), channel_id=1, source_target_pairs={{0,1},{1,2},{2,3},{3,4},{4,5},{5,6},{6,7},{8,9},{9,10},{10,11},{11... | collective-permute-start | bytes 1572872 | tf_op jit(solution)/shard_map/ppermute | solution.py:16
  26.8 1.7 copy-start.10
  26.9 1.7 copy-start.5
  28.7 1.4 copy-start.16
  30.9 35.5 %copy-start.3 = (f32[2,8,128,128]{3,2,1,0:T(8,128)}, f32[2,8,128,128]{3,2,1,0:T(8,128)S(1)}, u32[]{:S(2)}) copy-start(f32[2,8,128,128]{3,2,1,0:T(8,128)S(1)} %get-tuple-element.19) | copy-start | bytes 3145732
  31.0 4.9 %copy-start.11 = (f32[2,128,127]{2,1,0:T(8,128)S(1)}, f32[2,128,127]{2,1,0:T(8,128)}, u32[]{:S(2)}) copy-start(f32[2,128,127]{2,1,0:T(8,128)} %copy-done.10) | copy-start | bytes 390148
  31.0 5.3 %collective-permute-start.4 = (f32[1,8,128,128]{3,2,1,0:T(8,128)S(1)}, f32[1,8,128,128]{3,2,1,0:T(8,128)S(1)}, u32[]{:S(2)}, u32[]{:S(2)}) collective-permute-start(f32[1,8,128,128]{3,2,1,0:T(8,128)S(1)} %get-tuple-element.31), channel_id=1, source_target_pairs={{1,0},{2,1},{3,2},{4,3},{5,4},{6,5},{7,6},{9,8},{10,9},{11,10},{12... | collective-permute-start | bytes 1572872 | tf_op jit(solution)/shard_map/ppermute | solution.py:19
  32.5 3.7 %copy-start.6 = (f32[2,127,128]{2,1,0:T(8,128)S(1)}, f32[2,127,128]{2,1,0:T(8,128)}, u32[]{:S(2)}) copy-start(f32[2,127,128]{2,1,0:T(8,128)} %copy-done.5) | copy-start | bytes 390148
  32.5 4.8 %collective-permute-start.5 = (f32[1,8,128,128]{3,2,1,0:T(8,128)S(1)}, f32[1,8,128,128]{3,2,1,0:T(8,128)S(1)}, u32[]{:S(2)}, u32[]{:S(2)}) collective-permute-start(f32[1,8,128,128]{3,2,1,0:T(8,128)S(1)} %get-tuple-element.30), channel_id=1, source_target_pairs={{0,1},{1,2},{2,3},{3,4},{4,5},{5,6},{6,7},{8,9},{9,10},{10,11},{11... | collective-permute-start | bytes 1572872 | tf_op jit(solution)/shard_map/ppermute | solution.py:16
  68.0 26.5 %collective-permute-start.8 = (f32[1,8,128,128]{3,2,1,0:T(8,128)}, f32[1,8,128,128]{3,2,1,0:T(8,128)}, u32[]{:S(2)}, u32[]{:S(2)}) collective-permute-start(f32[1,8,128,128]{3,2,1,0:T(8,128)} %get-tuple-element.35), channel_id=1, source_target_pairs={{1,0},{2,1},{3,2},{4,3},{5,4},{6,5},{7,6},{9,8},{10,9},{11,10},{12... | collective-permute-start | bytes 1572872 | tf_op jit(solution)/shard_map/ppermute | solution.py:19
  87.0 4.6 %copy-start.12 = (f32[2,128,127]{2,1,0:T(8,128)S(1)}, f32[2,128,127]{2,1,0:T(8,128)}, u32[]{:S(2)}) copy-start(f32[2,128,127]{2,1,0:T(8,128)} %copy-done.10) | copy-start | bytes 390148
  87.1 7.4 %collective-permute-start.6 = (f32[1,8,128,128]{3,2,1,0:T(8,128)S(1)}, f32[1,8,128,128]{3,2,1,0:T(8,128)S(1)}, u32[]{:S(2)}, u32[]{:S(2)}) collective-permute-start(f32[1,8,128,128]{3,2,1,0:T(8,128)S(1)} %get-tuple-element.29), channel_id=1, source_target_pairs={{1,0},{2,1},{3,2},{4,3},{5,4},{6,5},{7,6},{9,8},{10,9},{11,10},{12... | collective-permute-start | bytes 1572872 | tf_op jit(solution)/shard_map/ppermute | solution.py:19
  88.4 4.8 %copy-start.7 = (f32[2,127,128]{2,1,0:T(8,128)S(1)}, f32[2,127,128]{2,1,0:T(8,128)}, u32[]{:S(2)}) copy-start(f32[2,127,128]{2,1,0:T(8,128)} %copy-done.5) | copy-start | bytes 390148
  88.4 6.1 %collective-permute-start.7 = (f32[1,8,128,128]{3,2,1,0:T(8,128)S(1)}, f32[1,8,128,128]{3,2,1,0:T(8,128)S(1)}, u32[]{:S(2)}, u32[]{:S(2)}) collective-permute-start(f32[1,8,128,128]{3,2,1,0:T(8,128)S(1)} %get-tuple-element.28), channel_id=1, source_target_pairs={{0,1},{1,2},{2,3},{3,4},{4,5},{5,6},{6,7},{8,9},{9,10},{10,11},{11... | collective-permute-start | bytes 1572872 | tf_op jit(solution)/shard_map/ppermute | solution.py:16
  118.6 15.3 %copy-start.19 = (f32[8]{0:T(128)S(1)}, f32[8]{0:T(128)}, u32[]{:S(2)}) copy-start(f32[8]{0:T(128)} %param.11) | copy-start | bytes 100
  133.9 3.8 %copy-start.20 = (f32[8]{0:T(128)}, f32[8]{0:T(128)S(1)}, u32[]{:S(2)}) copy-start(f32[8]{0:T(128)S(1)} %psum.74) | copy-start | bytes 100
  137.6 4.6 %copy-start.13 = (f32[2,128,127]{2,1,0:T(8,128)S(1)}, f32[2,128,127]{2,1,0:T(8,128)}, u32[]{:S(2)}) copy-start(f32[2,128,127]{2,1,0:T(8,128)} %copy-done.10) | copy-start | bytes 390148
  137.7 5.0 %collective-permute-start.10 = (f32[1,8,128,128]{3,2,1,0:T(8,128)S(1)}, f32[1,8,128,128]{3,2,1,0:T(8,128)S(1)}, u32[]{:S(2)}, u32[]{:S(2)}) collective-permute-start(f32[1,8,128,128]{3,2,1,0:T(8,128)S(1)} %get-tuple-element.27), channel_id=1, source_target_pairs={{1,0},{2,1},{3,2},{4,3},{5,4},{6,5},{7,6},{9,8},{10,9},{11,10},{12... | collective-permute-start | bytes 1572872 | tf_op jit(solution)/shard_map/ppermute | solution.py:19
  139.0 3.6 %copy-start.8 = (f32[2,127,128]{2,1,0:T(8,128)S(1)}, f32[2,127,128]{2,1,0:T(8,128)}, u32[]{:S(2)}) copy-start(f32[2,127,128]{2,1,0:T(8,128)} %copy-done.5) | copy-start | bytes 390148
  139.0 4.7 %collective-permute-start.11 = (f32[1,8,128,128]{3,2,1,0:T(8,128)S(1)}, f32[1,8,128,128]{3,2,1,0:T(8,128)S(1)}, u32[]{:S(2)}, u32[]{:S(2)}) collective-permute-start(f32[1,8,128,128]{3,2,1,0:T(8,128)S(1)} %get-tuple-element.26), channel_id=1, source_target_pairs={{0,1},{1,2},{2,3},{3,4},{4,5},{5,6},{6,7},{8,9},{9,10},{10,11},{11... | collective-permute-start | bytes 1572872 | tf_op jit(solution)/shard_map/ppermute | solution.py:16
  144.7 33.3 %copy-start.4 = (f32[2,8,128,128]{3,2,1,0:T(8,128)}, f32[2,8,128,128]{3,2,1,0:T(8,128)S(1)}, u32[]{:S(2)}) copy-start(f32[2,8,128,128]{3,2,1,0:T(8,128)S(1)} %get-tuple-element.12) | copy-start | bytes 3145732
  179.5 4.6 %copy-start.14 = (f32[2,128,127]{2,1,0:T(8,128)S(1)}, f32[2,128,127]{2,1,0:T(8,128)}, u32[]{:S(2)}) copy-start(f32[2,128,127]{2,1,0:T(8,128)} %copy-done.10) | copy-start | bytes 390148
  179.6 5.0 %collective-permute-start.12 = (f32[1,8,128,128]{3,2,1,0:T(8,128)S(1)}, f32[1,8,128,128]{3,2,1,0:T(8,128)S(1)}, u32[]{:S(2)}, u32[]{:S(2)}) collective-permute-start(f32[1,8,128,128]{3,2,1,0:T(8,128)S(1)} %get-tuple-element.25), channel_id=1, source_target_pairs={{1,0},{2,1},{3,2},{4,3},{5,4},{6,5},{7,6},{9,8},{10,9},{11,10},{12... | collective-permute-start | bytes 1572872 | tf_op jit(solution)/shard_map/ppermute | solution.py:19
  180.9 3.6 %copy-start.9 = (f32[2,127,128]{2,1,0:T(8,128)S(1)}, f32[2,127,128]{2,1,0:T(8,128)}, u32[]{:S(2)}) copy-start(f32[2,127,128]{2,1,0:T(8,128)} %copy-done.5) | copy-start | bytes 390148
  180.9 4.7 %collective-permute-start.13 = (f32[1,8,128,128]{3,2,1,0:T(8,128)S(1)}, f32[1,8,128,128]{3,2,1,0:T(8,128)S(1)}, u32[]{:S(2)}, u32[]{:S(2)}) collective-permute-start(f32[1,8,128,128]{3,2,1,0:T(8,128)S(1)} %get-tuple-element.24), channel_id=1, source_target_pairs={{0,1},{1,2},{2,3},{3,4},{4,5},{5,6},{6,7},{8,9},{9,10},{10,11},{11... | collective-permute-start | bytes 1572872 | tf_op jit(solution)/shard_map/ppermute | solution.py:16
  207.2 1.2 copy-start.2
  208.7 5.3 %collective-permute-start.14 = (f32[1,16,128,128]{3,2,1,0:T(8,128)S(1)}, f32[1,16,128,128]{3,2,1,0:T(8,128)S(1)}, u32[]{:S(2)}, u32[]{:S(2)}) collective-permute-start(f32[1,16,128,128]{3,2,1,0:T(8,128)S(1)} %get-tuple-element.22), channel_id=1, source_target_pairs={{1,0},{2,1},{3,2},{4,3},{5,4},{6,5},{7,6},{9,8},{10,9},{11,10},{12... | collective-permute-start | bytes 3145736 | tf_op jit(solution)/shard_map/ppermute | solution.py:19
  210.0 5.3 %collective-permute-start.15 = (f32[1,16,128,128]{3,2,1,0:T(8,128)S(1)}, f32[1,16,128,128]{3,2,1,0:T(8,128)S(1)}, u32[]{:S(2)}, u32[]{:S(2)}) collective-permute-start(f32[1,16,128,128]{3,2,1,0:T(8,128)S(1)} %get-tuple-element.23), channel_id=1, source_target_pairs={{0,1},{1,2},{2,3},{3,4},{4,5},{5,6},{6,7},{8,9},{9,10},{10,11},{11... | collective-permute-start | bytes 3145736 | tf_op jit(solution)/shard_map/ppermute | solution.py:16
Sparse Core Ops, SparseCore 0:
  217.8 56.2 all-reduce.35
where the time goes:
time: 283 us; the launch traced here: 282 us
  blocking collectives  130 us (46%)
  waiting for transfers between devices  60.6 us (21%)
  starting transfers between devices  39.3 us (14%)
  other arithmetic  31.2 us (11%)
  between operations  14.7 us (5%)
  local copies, waits for them, and re-layouts  7.01 us (2%)
    psum x6, blocking collectives, pattern_sum(): return lax.psum(local_terms, 'vox')  117 us
    psum x1, waiting for transfers between devices, per_device(): gradient = lax.psum(local_gradient, 'pat')  56.4 us
    ppermute x8, starting transfers between devices, extended(): lax.ppermute(lax.slice_in_dim(block, block.shape[dim] - width, None, axis...  28.6 us
    psum x1, blocking collectives, per_device(): predicted = lax.psum(inner(probe_weights, forward), 'vox')  12.4 us
    ppermute x8, starting transfers between devices, extended(): lax.ppermute(lax.slice_in_dim(block, 0, width, axis=dim), axis, backward)  10.6 us
    reduce_sum x7, other arithmetic, inner(): return jnp.sum(left_factor * right_factor, axis=(0, 2, 3))  8.68 us
  transfers between devices with their start and end apart: 17, of which 5 were waited for; matrix products, arithmetic and copies ran while one was open for 6% of the time, Pallas kernels for 0%

commit v1 on v0

--- a/solution.py
+++ b/solution.py
@@ -149,7 +149,8 @@
     local_gradient = -0.5 * (
         grad_depth + both_sides(row_products, 1) + both_sides(column_products, 2)
     )
-    gradient = lax.psum(local_gradient, "pat")
+    remake_table = lambda body: jnp.sum(jax.lax.all_gather(body, axis_name="pat"), axis=0)
+    gradient = remake_table(local_gradient)
     return (gradient, predicted)
 
 

time: 283 us -> 248 us (0.88)
  the two profiles are of different devices: /device:TPU:0 before, /device:TPU:4 now
where the time goes in v1:
time: 248 us; the launch traced here: 247 us
  blocking collectives  105 us (42%)
  waiting for transfers between devices  64.9 us (26%)
  starting transfers between devices  38.7 us (16%)
  other arithmetic  31.2 us (13%)
  local copies, waits for them, and re-layouts  5.45 us (2%)
    psum x6, blocking collectives, pattern_sum(): return lax.psum(local_terms, 'vox')  77.5 us
    ppermute x8, waiting for transfers between devices, extended(): lax.ppermute(lax.slice_in_dim(block, 0, width, axis=dim), axis, backward)  47.7 us
    ppermute x8, starting transfers between devices, extended(): lax.ppermute(lax.slice_in_dim(block, 0, width, axis=dim), axis, backward)  21.1 us
    ppermute x8, starting transfers between devices, extended(): lax.ppermute(lax.slice_in_dim(block, block.shape[dim] - width, None, axis...  17.6 us
    ppermute x8, waiting for transfers between devices, extended(): lax.ppermute(lax.slice_in_dim(block, block.shape[dim] - width, None, axis...  17.1 us
    all_gather x1, blocking collectives, per_device(): jax.lax.all_gather(body, axis_name='pat')  15.9 us
    psum x1, blocking collectives, per_device(): predicted = lax.psum(inner(probe_weights, forward), 'vox')  11.8 us
    reduce_sum x7, other arithmetic, inner(): return jnp.sum(left_factor * right_factor, axis=(0, 2, 3))  8.69 us
  transfers between devices with their start and end apart: 16, of which 12 were waited for; matrix products, arithmetic and copies ran while one was open for 7% of the time, Pallas kernels for 0%

profile of v1, /device:TPU:4, one launch (start us, length us, event | category | flops | bytes accessed | tf_op | source)
XLA Modules:
  0.0 246.7 jit_solution(10584825285196675312)
XLA Ops:
  1.6 2.8 %collective-permute-start = (f32[1,128,128]{2,1,0:T(8,128)S(1)}, f32[1,128,128]{2,1,0:T(8,128)S(1)}, u32[]{:S(2)}, u32[]{:S(2)}) collective-permute-start(f32[1,128,128]{2,1,0:T(8,128)S(1)} %get-tuple-element.43), channel_id=1, source_target_pairs={{1,0},{2,1},{3,2},{4,3},{5,4},{6,5},{7,6},{9,8},{10,9},{11,10},{12... | collective-permute-start | bytes 196616 | tf_op jit(solution)/shard_map/ppermute | solution.py:19
  4.4 1.9 collective-permute-start.1
  6.3 2.1 fusion.61
  8.4 4.7 %collective-permute-start.2 = (f32[1,8,128,128]{3,2,1,0:T(8,128)}, f32[1,8,128,128]{3,2,1,0:T(8,128)}, u32[]{:S(2)}, u32[]{:S(2)}) collective-permute-start(f32[1,8,128,128]{3,2,1,0:T(8,128)} %get-tuple-element.33), channel_id=1, source_target_pairs={{1,0},{2,1},{3,2},{4,3},{5,4},{6,5},{7,6},{9,8},{10,9},{11,10},{12... | collective-permute-start | bytes 1572872 | tf_op jit(solution)/shard_map/ppermute | solution.py:19
  13.1 1.9 collective-permute-start.3
  15.0 1.1 fusion.62
  16.1 1.9 collective-permute-start.9
  20.0 4.8 %collective-permute-done.2 = f32[1,8,128,128]{3,2,1,0:T(8,128)} collective-permute-done((f32[1,8,128,128]{3,2,1,0:T(8,128)}, f32[1,8,128,128]{3,2,1,0:T(8,128)}, u32[]{:S(2)}, u32[]{:S(2)}) %collective-permute-start.2) | collective-permute-done | bytes 524320 | tf_op jit(solution)/shard_map/ppermute | solution.py:19
  24.9 1.0 collective-permute-done.3
  25.8 1.3 fusion.2
  28.1 3.9 %collective-permute-start.4 = (f32[1,8,128,128]{3,2,1,0:T(8,128)S(1)}, f32[1,8,128,128]{3,2,1,0:T(8,128)S(1)}, u32[]{:S(2)}, u32[]{:S(2)}) collective-permute-start(f32[1,8,128,128]{3,2,1,0:T(8,128)S(1)} %get-tuple-element.31), channel_id=1, source_target_pairs={{1,0},{2,1},{3,2},{4,3},{5,4},{6,5},{7,6},{9,8},{10,9},{11,10},{12... | collective-permute-start | bytes 1572872 | tf_op jit(solution)/shard_map/ppermute | solution.py:19
  32.0 2.1 collective-permute-start.5
  34.6 7.7 %collective-permute-done.4 = f32[1,8,128,128]{3,2,1,0:T(8,128)S(1)} collective-permute-done((f32[1,8,128,128]{3,2,1,0:T(8,128)S(1)}, f32[1,8,128,128]{3,2,1,0:T(8,128)S(1)}, u32[]{:S(2)}, u32[]{:S(2)}) %collective-permute-start.4) | collective-permute-done | bytes 524320 | tf_op jit(solution)/shard_map/ppermute | solution.py:19
  42.3 1.3 collective-permute-done.5
  43.7 1.7 multiply_reduce_fusion.5
  45.4 13.3 %all-reduce.33 = (f32[8]{0:T(128)S(1)}, f32[8]{0:T(128)S(1)}) all-reduce(f32[8]{0:T(128)S(1)} %get-tuple-element.5, f32[8]{0:T(128)S(1)} %get-tuple-element.4), channel_id=1, replica_groups=mesh['pat'=4,'vox'=8] {'vox'}, use_global_device_ids=true, to_apply=%region_2.3 | all-reduce | flops 16 | bytes 128 | tf_op jit(solution)/shard_map/psum | solution.py:61
  58.7 1.6 multiply_reduce_fusion.4
  60.3 1.9 collective-permute-start.8
  62.2 16.4 %psum.65 = f32[8]{0:T(128)S(1)} all-reduce(f32[8]{0:T(128)S(1)} %multiply_reduce_fusion.4), channel_id=1, replica_groups=mesh['pat'=4,'vox'=8] {'vox'}, use_global_device_ids=true, to_apply=%region_6.7 | all-reduce | flops 8 | bytes 64 | tf_op jit(solution)/shard_map/psum | solution.py:61
  78.7 1.8 multiply_add_fusion.3
  80.6 1.9 collective-permute-start.6
  82.5 2.5 %collective-permute-start.7 = (f32[1,8,128,128]{3,2,1,0:T(8,128)S(1)}, f32[1,8,128,128]{3,2,1,0:T(8,128)S(1)}, u32[]{:S(2)}, u32[]{:S(2)}) collective-permute-start(f32[1,8,128,128]{3,2,1,0:T(8,128)S(1)} %get-tuple-element.28), channel_id=1, source_target_pairs={{0,1},{1,2},{2,3},{3,4},{4,5},{5,6},{6,7},{8,9},{9,10},{10,11},{11... | collective-permute-start | bytes 1572872 | tf_op jit(solution)/shard_map/ppermute | solution.py:16
  85.1 1.6 fusion.29
  86.7 1.3 fusion.30
  87.9 5.0 %collective-permute-done.6 = f32[1,8,128,128]{3,2,1,0:T(8,128)S(1)} collective-permute-done((f32[1,8,128,128]{3,2,1,0:T(8,128)S(1)}, f32[1,8,128,128]{3,2,1,0:T(8,128)S(1)}, u32[]{:S(2)}, u32[]{:S(2)}) %collective-permute-start.6) | collective-permute-done | bytes 524320 | tf_op jit(solution)/shard_map/ppermute | solution.py:19
  92.9 2.1 collective-permute-done.7
  95.0 2.8 %fusion.4 = (f32[3,8,128,128]{3,2,1,0:T(8,128)S(1)}, f32[3,8,128,128]{3,2,1,0:T(8,128)}) fusion(f32[1,8,128,128]{3,2,1,0:T(8,128)S(1)} %collective-permute-done.6, f32[2,8,128,128]{3,2,1,0:T(8,128)S(1)} %multiply_add_fusion.3, f32[1,8,128,128]{3,2,1,0:T(8,128)S(1)} %collective-permute-done.7, f32[3,128,128]{2,1,0:T(8,128)S(1)} %fusion.45, ...), kind=kLoop, calls=%fused_computation.13 | loop fusion | flops 3145728 | bytes 7536640 | tf_op jit(solution)/shard_map/mul | solution.py:43
  98.5 12.5 %psum.66 = f32[8]{0:T(128)S(1)} all-reduce(f32[8]{0:T(128)S(1)} %fusion.35), channel_id=1, replica_groups=mesh['pat'=4,'vox'=8] {'vox'}, use_global_device_ids=true, to_apply=%region_8.9 | all-reduce | flops 8 | bytes 64 | tf_op jit(solution)/shard_map/psum | solution.py:61
  111.0 2.8 %multiply_reduce_fusion.3 = (f32[8]{0:T(128)S(1)}, f32[2,8,128,128]{3,2,1,0:T(8,128)}) fusion(s32[2,128,128]{2,1,0:T(8,128)} %iota_add_fusion, s32[8]{0:T(128)S(1)} %get-tuple-element.45, s32[8]{0:T(128)S(1)} %get-tuple-element.46, f32[2,8,128,128]{3,2,1,0:T(8,128)S(1)} %multiply_add_fusion.3, f32[8]{0:T(128)S(1)} %div.49, ...), kind=kLoop, calls=%fused_computation.84 | loop fusion | flops 3145720 | bytes 4456608 | tf_op jit(solution)/shard_map/reduce_sum | solution.py:53
  113.8 11.8 %psum.67 = f32[8]{0:T(128)S(1)} all-reduce(f32[8]{0:T(128)S(1)} %get-tuple-element.15), channel_id=1, replica_groups=mesh['pat'=4,'vox'=8] {'vox'}, use_global_device_ids=true, to_apply=%region_10.11 | all-reduce | flops 8 | bytes 64 | tf_op jit(solution)/shard_map/psum | solution.py:126
  125.6 3.7 %broadcast_divide_fusion = (f32[2,8,128,128]{3,2,1,0:T(8,128)S(1)}, f32[2,8,128,128]{3,2,1,0:T(8,128)S(1)}) fusion(f32[2,128,128]{2,1,0:T(8,128)S(1)} %fusion.51, f32[2,8,128,127]{3,2,1,0:T(8,128)} %get-tuple-element.41, f32[2,8,127,128]{3,2,1,0:T(8,128)} %get-tuple-element.39, f32[3,8,128,128]{3,2,1,0:T(8,128)} %get-tuple-element.37, ...), kind=kLoop, calls=%fused_computation.94 | loop fusion | flops 3932160 | bytes 7585888 | tf_op jit(solution)/shard_map/div | solution.py:67
  129.5 1.9 collective-permute-start.10
  131.4 2.5 %collective-permute-start.11 = (f32[1,8,128,128]{3,2,1,0:T(8,128)S(1)}, f32[1,8,128,128]{3,2,1,0:T(8,128)S(1)}, u32[]{:S(2)}, u32[]{:S(2)}) collective-permute-start(f32[1,8,128,128]{3,2,1,0:T(8,128)S(1)} %get-tuple-element.26), channel_id=1, source_target_pairs={{0,1},{1,2},{2,3},{3,4},{4,5},{5,6},{6,7},{8,9},{9,10},{10,11},{11... | collective-permute-start | bytes 1572872 | tf_op jit(solution)/shard_map/ppermute | solution.py:16
  134.5 6.2 %collective-permute-done.10 = f32[1,8,128,128]{3,2,1,0:T(8,128)S(1)} collective-permute-done((f32[1,8,128,128]{3,2,1,0:T(8,128)S(1)}, f32[1,8,128,128]{3,2,1,0:T(8,128)S(1)}, u32[]{:S(2)}, u32[]{:S(2)}) %collective-permute-start.10) | collective-permute-done | bytes 524320 | tf_op jit(solution)/shard_map/ppermute | solution.py:19
  140.7 4.4 %collective-permute-done.11 = f32[1,8,128,128]{3,2,1,0:T(8,128)S(1)} collective-permute-done((f32[1,8,128,128]{3,2,1,0:T(8,128)S(1)}, f32[1,8,128,128]{3,2,1,0:T(8,128)S(1)}, u32[]{:S(2)}, u32[]{:S(2)}) %collective-permute-start.11) | collective-permute-done | bytes 524320 | tf_op jit(solution)/shard_map/ppermute | solution.py:16
  146.1 11.8 %all-reduce.32 = (f32[8]{0:T(128)S(1)}, f32[8]{0:T(128)S(1)}) all-reduce(f32[8]{0:T(128)S(1)} %get-tuple-element.3, f32[8]{0:T(128)S(1)} %get-tuple-element.2), channel_id=1, replica_groups=mesh['pat'=4,'vox'=8] {'vox'}, use_global_device_ids=true, to_apply=%region_12.13 | all-reduce | flops 16 | bytes 128 | tf_op jit(solution)/shard_map/psum | solution.py:61
  158.3 11.8 %psum.70 = f32[8]{0:T(128)S(1)} all-reduce(f32[8]{0:T(128)S(1)} %multiply_reduce_fusion), channel_id=1, replica_groups=mesh['pat'=4,'vox'=8] {'vox'}, use_global_device_ids=true, to_apply=%region_16.17 | all-reduce | flops 8 | bytes 64 | tf_op jit(solution)/shard_map/psum | solution.py:61
  170.1 1.5 multiply_add_fusion.1
  171.7 2.1 collective-permute-start.12
  173.8 2.4 collective-permute-start.13
  176.7 6.6 %collective-permute-done.12 = f32[1,8,128,128]{3,2,1,0:T(8,128)S(1)} collective-permute-done((f32[1,8,128,128]{3,2,1,0:T(8,128)S(1)}, f32[1,8,128,128]{3,2,1,0:T(8,128)S(1)}, u32[]{:S(2)}, u32[]{:S(2)}) %collective-permute-start.12) | collective-permute-done | bytes 524320 | tf_op jit(solution)/shard_map/ppermute | solution.py:19
  183.3 3.5 %collective-permute-done.13 = f32[1,8,128,128]{3,2,1,0:T(8,128)S(1)} collective-permute-done((f32[1,8,128,128]{3,2,1,0:T(8,128)S(1)}, f32[1,8,128,128]{3,2,1,0:T(8,128)S(1)}, u32[]{:S(2)}, u32[]{:S(2)}) %collective-permute-start.13) | collective-permute-done | bytes 524320 | tf_op jit(solution)/shard_map/ppermute | solution.py:16
  187.7 11.8 %psum.71 = f32[8]{0:T(128)S(1)} all-reduce(f32[8]{0:T(128)S(1)} %fusion.19), channel_id=1, replica_groups=mesh['pat'=4,'vox'=8] {'vox'}, use_global_device_ids=true, to_apply=%region_18.19 | all-reduce | flops 8 | bytes 64 | tf_op jit(solution)/shard_map/psum | solution.py:61
  201.0 1.9 collective-permute-start.14
  202.9 2.4 collective-permute-start.15
  206.2 17.4 %collective-permute-done.14 = f32[1,16,128,128]{3,2,1,0:T(8,128)S(1)} collective-permute-done((f32[1,16,128,128]{3,2,1,0:T(8,128)S(1)}, f32[1,16,128,128]{3,2,1,0:T(8,128)S(1)}, u32[]{:S(2)}, u32[]{:S(2)}) %collective-permute-start.14) | collective-permute-done | bytes 1048608 | tf_op jit(solution)/shard_map/ppermute | solution.py:19
  223.6 4.9 %collective-permute-done.15 = f32[1,16,128,128]{3,2,1,0:T(8,128)S(1)} collective-permute-done((f32[1,16,128,128]{3,2,1,0:T(8,128)S(1)}, f32[1,16,128,128]{3,2,1,0:T(8,128)S(1)}, u32[]{:S(2)}, u32[]{:S(2)}) %collective-permute-start.15) | collective-permute-done | bytes 1048608 | tf_op jit(solution)/shard_map/ppermute | solution.py:16
  230.2 15.9 %all-gather = f32[8,128,128]{2,1,0:T(8,128)S(1)} all-gather(f32[2,128,128]{2,1,0:T(8,128)S(1)} %fusion.48), channel_id=2, replica_groups=mesh['pat'=4,'vox'=8] {'pat'}, dimensions={0}, use_global_device_ids=true | all-gather | bytes 655360 | tf_op jit(solution)/shard_map/all_gather | solution.py:152
  (94 shorter events, 13.4 us)
Async XLA Ops:
  0.6 14.4 %copy-start = (f32[2,8,128,128]{3,2,1,0:T(8,128)S(1)}, f32[2,8,128,128]{3,2,1,0:T(8,128)}, u32[]{:S(2)}) copy-start(f32[2,8,128,128]{3,2,1,0:T(8,128)} %param.8) | copy-start | bytes 3145732
  1.6 18.2 %collective-permute-start = (f32[1,128,128]{2,1,0:T(8,128)S(1)}, f32[1,128,128]{2,1,0:T(8,128)S(1)}, u32[]{:S(2)}, u32[]{:S(2)}) collective-permute-start(f32[1,128,128]{2,1,0:T(8,128)S(1)} %get-tuple-element.43), channel_id=1, source_target_pairs={{1,0},{2,1},{3,2},{4,3},{5,4},{6,5},{7,6},{9,8},{10,9},{11,10},{12... | collective-permute-start | bytes 196616 | tf_op jit(solution)/shard_map/ppermute | solution.py:19
  4.4 15.4 %collective-permute-start.1 = (f32[1,128,128]{2,1,0:T(8,128)S(1)}, f32[1,128,128]{2,1,0:T(8,128)S(1)}, u32[]{:S(2)}, u32[]{:S(2)}) collective-permute-start(f32[1,128,128]{2,1,0:T(8,128)S(1)} %get-tuple-element.42), channel_id=1, source_target_pairs={{0,1},{1,2},{2,3},{3,4},{4,5},{5,6},{6,7},{8,9},{9,10},{10,11},{11... | collective-permute-start | bytes 196616 | tf_op jit(solution)/shard_map/ppermute | solution.py:16
  8.4 9.6 %copy-start.15 = (f32[2,128,128]{2,1,0:T(8,128)S(1)}, f32[2,128,128]{2,1,0:T(8,128)}, u32[]{:S(2)}) copy-start(f32[2,128,128]{2,1,0:T(8,128)} %param.6) | copy-start | bytes 393220
  8.4 10.5 %copy-start.17 = (s32[8,4]{0,1:T(4,128)S(1)}, s32[8,4]{0,1:T(4,128)}, u32[]{:S(2)}) copy-start(s32[8,4]{0,1:T(4,128)} %param.10) | copy-start | bytes 388
  8.4 10.5 %copy-start.18 = (s32[128]{0:T(128)S(1)}, s32[128]{0:T(128)}, u32[]{:S(2)}) copy-start(s32[128]{0:T(128)} %param.9) | copy-start | bytes 1540
  8.4 10.8 %copy-start.1 = (f32[2,8,128,128]{3,2,1,0:T(8,128)S(1)}, f32[2,8,128,128]{3,2,1,0:T(8,128)}, u32[]{:S(2)}) copy-start(f32[2,8,128,128]{3,2,1,0:T(8,128)} %param.7) | copy-start | bytes 3145732
  8.4 16.4 %collective-permute-start.2 = (f32[1,8,128,128]{3,2,1,0:T(8,128)}, f32[1,8,128,128]{3,2,1,0:T(8,128)}, u32[]{:S(2)}, u32[]{:S(2)}) collective-permute-start(f32[1,8,128,128]{3,2,1,0:T(8,128)} %get-tuple-element.33), channel_id=1, source_target_pairs={{1,0},{2,1},{3,2},{4,3},{5,4},{6,5},{7,6},{9,8},{10,9},{11,10},{12... | collective-permute-start | bytes 1572872 | tf_op jit(solution)/shard_map/ppermute | solution.py:19
  13.1 12.7 %collective-permute-start.3 = (f32[1,8,128,128]{3,2,1,0:T(8,128)S(1)}, f32[1,8,128,128]{3,2,1,0:T(8,128)}, u32[]{:S(2)}, u32[]{:S(2)}) collective-permute-start(f32[1,8,128,128]{3,2,1,0:T(8,128)S(1)} %get-tuple-element.32), channel_id=1, source_target_pairs={{0,1},{1,2},{2,3},{3,4},{4,5},{5,6},{6,7},{8,9},{9,10},{10,11},{11... | collective-permute-start | bytes 1572872 | tf_op jit(solution)/shard_map/ppermute | solution.py:16
  16.1 71.8 %collective-permute-start.9 = (f32[1,8,128,128]{3,2,1,0:T(8,128)}, f32[1,8,128,128]{3,2,1,0:T(8,128)}, u32[]{:S(2)}, u32[]{:S(2)}) collective-permute-start(f32[1,8,128,128]{3,2,1,0:T(8,128)} %get-tuple-element.34), channel_id=1, source_target_pairs={{0,1},{1,2},{2,3},{3,4},{4,5},{5,6},{6,7},{8,9},{9,10},{10,11},{11... | collective-permute-start | bytes 1572872 | tf_op jit(solution)/shard_map/ppermute | solution.py:16
  18.2 1.7 copy-start.10
  18.2 1.7 copy-start.5
  20.0 7.2 %copy-start.16 = (s32[2,128,128]{2,1,0:T(8,128)S(1)}, s32[2,128,128]{2,1,0:T(8,128)}, u32[]{:S(2)}) copy-start(s32[2,128,128]{2,1,0:T(8,128)} %iota_add_fusion) | copy-start | bytes 393220
  28.0 30.7 %copy-start.3 = (f32[2,8,128,128]{3,2,1,0:T(8,128)}, f32[2,8,128,128]{3,2,1,0:T(8,128)S(1)}, u32[]{:S(2)}) copy-start(f32[2,8,128,128]{3,2,1,0:T(8,128)S(1)} %get-tuple-element.19) | copy-start | bytes 3145732
  28.0 6.0 %copy-start.11 = (f32[2,128,127]{2,1,0:T(8,128)S(1)}, f32[2,128,127]{2,1,0:T(8,128)}, u32[]{:S(2)}) copy-start(f32[2,128,127]{2,1,0:T(8,128)} %copy-done.10) | copy-start | bytes 390148
  28.1 14.1 %collective-permute-start.4 = (f32[1,8,128,128]{3,2,1,0:T(8,128)S(1)}, f32[1,8,128,128]{3,2,1,0:T(8,128)S(1)}, u32[]{:S(2)}, u32[]{:S(2)}) collective-permute-start(f32[1,8,128,128]{3,2,1,0:T(8,128)S(1)} %get-tuple-element.31), channel_id=1, source_target_pairs={{1,0},{2,1},{3,2},{4,3},{5,4},{6,5},{7,6},{9,8},{10,9},{11,10},{12... | collective-permute-start | bytes 1572872 | tf_op jit(solution)/shard_map/ppermute | solution.py:19
  32.0 2.4 copy-start.6
  32.0 11.5 %collective-permute-start.5 = (f32[1,8,128,128]{3,2,1,0:T(8,128)S(1)}, f32[1,8,128,128]{3,2,1,0:T(8,128)S(1)}, u32[]{:S(2)}, u32[]{:S(2)}) collective-permute-start(f32[1,8,128,128]{3,2,1,0:T(8,128)S(1)} %get-tuple-element.30), channel_id=1, source_target_pairs={{0,1},{1,2},{2,3},{3,4},{4,5},{5,6},{6,7},{8,9},{9,10},{10,11},{11... | collective-permute-start | bytes 1572872 | tf_op jit(solution)/shard_map/ppermute | solution.py:16
  60.3 27.6 %collective-permute-start.8 = (f32[1,8,128,128]{3,2,1,0:T(8,128)}, f32[1,8,128,128]{3,2,1,0:T(8,128)}, u32[]{:S(2)}, u32[]{:S(2)}) collective-permute-start(f32[1,8,128,128]{3,2,1,0:T(8,128)} %get-tuple-element.35), channel_id=1, source_target_pairs={{1,0},{2,1},{3,2},{4,3},{5,4},{6,5},{7,6},{9,8},{10,9},{11,10},{12... | collective-permute-start | bytes 1572872 | tf_op jit(solution)/shard_map/ppermute | solution.py:19
  80.5 4.6 %copy-start.12 = (f32[2,128,127]{2,1,0:T(8,128)S(1)}, f32[2,128,127]{2,1,0:T(8,128)}, u32[]{:S(2)}) copy-start(f32[2,128,127]{2,1,0:T(8,128)} %copy-done.10) | copy-start | bytes 390148
  80.6 12.3 %collective-permute-start.6 = (f32[1,8,128,128]{3,2,1,0:T(8,128)S(1)}, f32[1,8,128,128]{3,2,1,0:T(8,128)S(1)}, u32[]{:S(2)}, u32[]{:S(2)}) collective-permute-start(f32[1,8,128,128]{3,2,1,0:T(8,128)S(1)} %get-tuple-element.29), channel_id=1, source_target_pairs={{1,0},{2,1},{3,2},{4,3},{5,4},{6,5},{7,6},{9,8},{10,9},{11,10},{12... | collective-permute-start | bytes 1572872 | tf_op jit(solution)/shard_map/ppermute | solution.py:19
  82.5 4.2 %copy-start.7 = (f32[2,127,128]{2,1,0:T(8,128)S(1)}, f32[2,127,128]{2,1,0:T(8,128)}, u32[]{:S(2)}) copy-start(f32[2,127,128]{2,1,0:T(8,128)} %copy-done.5) | copy-start | bytes 390148
  82.5 12.5 %collective-permute-start.7 = (f32[1,8,128,128]{3,2,1,0:T(8,128)S(1)}, f32[1,8,128,128]{3,2,1,0:T(8,128)S(1)}, u32[]{:S(2)}, u32[]{:S(2)}) collective-permute-start(f32[1,8,128,128]{3,2,1,0:T(8,128)S(1)} %get-tuple-element.28), channel_id=1, source_target_pairs={{0,1},{1,2},{2,3},{3,4},{4,5},{5,6},{6,7},{8,9},{9,10},{10,11},{11... | collective-permute-start | bytes 1572872 | tf_op jit(solution)/shard_map/ppermute | solution.py:16
  111.0 14.6 %copy-start.19 = (f32[8]{0:T(128)S(1)}, f32[8]{0:T(128)}, u32[]{:S(2)}) copy-start(f32[8]{0:T(128)} %param.11) | copy-start | bytes 100
  125.6 3.8 %copy-start.20 = (f32[8]{0:T(128)}, f32[8]{0:T(128)S(1)}, u32[]{:S(2)}) copy-start(f32[8]{0:T(128)S(1)} %psum.67) | copy-start | bytes 100
  129.4 4.6 %copy-start.13 = (f32[2,128,127]{2,1,0:T(8,128)S(1)}, f32[2,128,127]{2,1,0:T(8,128)}, u32[]{:S(2)}) copy-start(f32[2,128,127]{2,1,0:T(8,128)} %copy-done.10) | copy-start | bytes 390148
  129.5 11.3 %collective-permute-start.10 = (f32[1,8,128,128]{3,2,1,0:T(8,128)S(1)}, f32[1,8,128,128]{3,2,1,0:T(8,128)S(1)}, u32[]{:S(2)}, u32[]{:S(2)}) collective-permute-start(f32[1,8,128,128]{3,2,1,0:T(8,128)S(1)} %get-tuple-element.27), channel_id=1, source_target_pairs={{1,0},{2,1},{3,2},{4,3},{5,4},{6,5},{7,6},{9,8},{10,9},{11,10},{12... | collective-permute-start | bytes 1572872 | tf_op jit(solution)/shard_map/ppermute | solution.py:19
  131.4 2.9 %copy-start.8 = (f32[2,127,128]{2,1,0:T(8,128)S(1)}, f32[2,127,128]{2,1,0:T(8,128)}, u32[]{:S(2)}) copy-start(f32[2,127,128]{2,1,0:T(8,128)} %copy-done.5) | copy-start | bytes 390148
  131.4 13.7 %collective-permute-start.11 = (f32[1,8,128,128]{3,2,1,0:T(8,128)S(1)}, f32[1,8,128,128]{3,2,1,0:T(8,128)S(1)}, u32[]{:S(2)}, u32[]{:S(2)}) collective-permute-start(f32[1,8,128,128]{3,2,1,0:T(8,128)S(1)} %get-tuple-element.26), channel_id=1, source_target_pairs={{0,1},{1,2},{2,3},{3,4},{4,5},{5,6},{6,7},{8,9},{9,10},{10,11},{11... | collective-permute-start | bytes 1572872 | tf_op jit(solution)/shard_map/ppermute | solution.py:16
  146.1 24.0 %copy-start.4 = (f32[2,8,128,128]{3,2,1,0:T(8,128)}, f32[2,8,128,128]{3,2,1,0:T(8,128)S(1)}, u32[]{:S(2)}) copy-start(f32[2,8,128,128]{3,2,1,0:T(8,128)S(1)} %get-tuple-element.12) | copy-start | bytes 3145732
  171.6 4.6 %copy-start.14 = (f32[2,128,127]{2,1,0:T(8,128)S(1)}, f32[2,128,127]{2,1,0:T(8,128)}, u32[]{:S(2)}) copy-start(f32[2,128,127]{2,1,0:T(8,128)} %copy-done.10) | copy-start | bytes 390148
  171.7 11.6 %collective-permute-start.12 = (f32[1,8,128,128]{3,2,1,0:T(8,128)S(1)}, f32[1,8,128,128]{3,2,1,0:T(8,128)S(1)}, u32[]{:S(2)}, u32[]{:S(2)}) collective-permute-start(f32[1,8,128,128]{3,2,1,0:T(8,128)S(1)} %get-tuple-element.25), channel_id=1, source_target_pairs={{1,0},{2,1},{3,2},{4,3},{5,4},{6,5},{7,6},{9,8},{10,9},{11,10},{12... | collective-permute-start | bytes 1572872 | tf_op jit(solution)/shard_map/ppermute | solution.py:19
  173.8 2.7 %copy-start.9 = (f32[2,127,128]{2,1,0:T(8,128)S(1)}, f32[2,127,128]{2,1,0:T(8,128)}, u32[]{:S(2)}) copy-start(f32[2,127,128]{2,1,0:T(8,128)} %copy-done.5) | copy-start | bytes 390148
  173.8 13.0 %collective-permute-start.13 = (f32[1,8,128,128]{3,2,1,0:T(8,128)S(1)}, f32[1,8,128,128]{3,2,1,0:T(8,128)S(1)}, u32[]{:S(2)}, u32[]{:S(2)}) collective-permute-start(f32[1,8,128,128]{3,2,1,0:T(8,128)S(1)} %get-tuple-element.24), channel_id=1, source_target_pairs={{0,1},{1,2},{2,3},{3,4},{4,5},{5,6},{6,7},{8,9},{9,10},{10,11},{11... | collective-permute-start | bytes 1572872 | tf_op jit(solution)/shard_map/ppermute | solution.py:16
  199.5 1.2 copy-start.2
  201.0 22.6 %collective-permute-start.14 = (f32[1,16,128,128]{3,2,1,0:T(8,128)S(1)}, f32[1,16,128,128]{3,2,1,0:T(8,128)S(1)}, u32[]{:S(2)}, u32[]{:S(2)}) collective-permute-start(f32[1,16,128,128]{3,2,1,0:T(8,128)S(1)} %get-tuple-element.22), channel_id=1, source_target_pairs={{1,0},{2,1},{3,2},{4,3},{5,4},{6,5},{7,6},{9,8},{10,9},{11,10},{12... | collective-permute-start | bytes 3145736 | tf_op jit(solution)/shard_map/ppermute | solution.py:19
  202.9 25.6 %collective-permute-start.15 = (f32[1,16,128,128]{3,2,1,0:T(8,128)S(1)}, f32[1,16,128,128]{3,2,1,0:T(8,128)S(1)}, u32[]{:S(2)}, u32[]{:S(2)}) collective-permute-start(f32[1,16,128,128]{3,2,1,0:T(8,128)S(1)} %get-tuple-element.23), channel_id=1, source_target_pairs={{0,1},{1,2},{2,3},{3,4},{4,5},{5,6},{6,7},{8,9},{9,10},{10,11},{11... | collective-permute-start | bytes 3145736 | tf_op jit(solution)/shard_map/ppermute | solution.py:16
